TPU v7x, 32 devices: a whole 2x2x4 slice. The times are simulated.
32 devices in a mesh: pole: 4 (over x, core), row: 4 (over z), col: 2 (over y).
Axes of the slice: x: 2, y: 2, z: 4, core: 2. Of those that a mesh axis runs over, the one named last changes fastest.
Arguments:
- green: bfloat16 [4, 4096, 4096], P('pole', 'row', 'col'), may hold values from -6 to 6
- factor: bfloat16 [4, 4096, 1024], P('pole', 'row', 'col'), may hold values from -0.09375 to 0.09375
- diag_inverse: bfloat16 [4, 512, 1024], P('pole', 'row', 'col'), may hold values from -6 to 6
- pole_weight: float32 [4], P('pole'), may hold values from 0.25 to 1
- pattern: int32 [8, 2], replicated, may hold values 0 or 1
Outputs:
- off_density: float32 [4096, 1024], P(('row', 'pole'), 'col')
- diag_density: float32 [512, 1024], P(('pole', 'row'), 'col')
All inputs are finite; a program needn't handle non-finite values.
Results may differ from a plain program's by a relative error of at most 0.005.
Values may be sent and summed in bfloat16 or wider, within the bound.
No kernel may reach another device: no remote copies, remote signals or barrier semaphores. Data moves between devices by JAX's collectives and lax.ppermute only.
A program may use at most 64 MiB of HBM per device.

v0:
```python
import jax
import jax.numpy as jnp
from jax import lax
from jax.sharding import PartitionSpec as P

BLOCK = 512
ANC = 8


def body(green, factor, diag_inverse, pole_weight, pattern):
    poles_here = green.shape[0]
    local_rows = factor.shape[1]
    local_cols = factor.shape[2]
    level_count = pattern.shape[1]
    row_at = lax.axis_index("row")
    col_at = lax.axis_index("col")
    row_ids = (row_at * local_rows + jnp.arange(local_rows, dtype=jnp.int32)) // BLOCK
    col_ids = (col_at * local_cols + jnp.arange(local_cols, dtype=jnp.int32)) // BLOCK
    row_onehot = (row_ids[:, None] == jnp.arange(ANC, dtype=jnp.int32)[None, :]).astype(jnp.float32)
    col_onehot = (col_ids[:, None] == jnp.arange(level_count, dtype=jnp.int32)[None, :]).astype(
        jnp.float32
    )
    pattern_f = pattern.astype(jnp.float32)
    keep_mask = jnp.dot(jnp.dot(row_onehot, pattern_f), col_onehot.T)
    masked = factor * keep_mask.astype(jnp.bfloat16)[None]
    whole_rows = lax.all_gather(green, "col", axis=2, tiled=True)
    product = jnp.einsum(
        "pij,pjk->pik",
        whole_rows,
        lax.all_gather(masked, "row", axis=1, tiled=True),
        preferred_element_type=jnp.float32,
    )
    update = (product * keep_mask[None]).astype(jnp.bfloat16)
    weights = pole_weight[:, None, None]
    off_term = -jnp.sum(weights * update.astype(jnp.float32), axis=0)
    level_here = local_cols // BLOCK
    factor_split = masked.reshape(poles_here, local_rows, level_here, BLOCK)
    update_split = update.reshape(poles_here, local_rows, level_here, BLOCK)
    cross_term = jnp.einsum(
        "prka,prkb->pakb", factor_split, update_split, preferred_element_type=jnp.float32
    )
    cross_term = cross_term.reshape(poles_here, BLOCK, local_cols)
    diag_term = -jnp.sum(weights * cross_term, axis=0)
    dinv_count = diag_inverse.shape[1]
    dinv_rows = jnp.sum(weights * diag_inverse.astype(jnp.float32), axis=0)
    current = lax.dynamic_slice_in_dim(diag_term, row_at * dinv_count, dinv_count, 0)
    diag_term = lax.dynamic_update_slice_in_dim(
        diag_term, current + dinv_rows, row_at * dinv_count, 0
    )
    off_density, pole_part = (
        lax.psum_scatter(off_term, "pole", scatter_dimension=0, tiled=True),
        lax.psum_scatter(diag_term, "pole", scatter_dimension=0, tiled=True),
    )
    diag_density = lax.psum_scatter(pole_part, "row", scatter_dimension=0, tiled=True)
    return (off_density, diag_density)


def solution(mesh):
    in_specs = (
        P("pole", "row", "col"),
        P("pole", "row", "col"),
        P("pole", "row", "col"),
        P("pole"),
        P(),
    )
    out_specs = (P(("row", "pole"), "col"), P(("pole", "row"), "col"))
    return jax.shard_map(body, mesh=mesh, in_specs=in_specs, out_specs=out_specs, check_vma=False)
```

profile of v0, /device:TPU:0, one launch (start us, length us, event | category | flops | bytes accessed | tf_op | source)
XLA Modules:
  0.0 296.8 jit_solution(12370110417123104437)
XLA Ops:
  7.2 0.0 all-gather.3.cloned.1.call-start
  7.3 2.9 bitcast_multiply_fusion.1
  10.1 0.0 all-gather.3.cloned.1.call-update
  10.2 0.0 copy-start.2
  10.2 0.0 all-gather.5.cloned.1.call-start
  10.2 0.7 all-gather.5.cloned.1.call-update
  10.9 0.0 reduce-scatter.8.cloned.1.call-start
  11.6 0.0 copy-done.2
  11.6 0.1 copy.11
  11.8 82.0 %all-gather.3.cloned.1.call-done = bf16[1,4096,512]{2,1,0:T(8,128)(2,1)} async-done(((bf16[1,1024,512]{2,1,0:T(8,128)(2,1)}), bf16[1,4096,512]{2,1,0:T(8,128)(2,1)}) %all-gather.3.cloned.1.call-update) | async-done | bytes 4194320 | tf_op jit(solution)/shard_map/all_gather | solution.py:30
  93.8 104.0 %all-gather.5.cloned.1.call-done = bf16[1,1024,4096]{2,1,0:T(8,128)(2,1)} async-done(((bf16[1,1024,2048]{2,1,0:T(8,128)(2,1)}), bf16[1,1024,4096]{2,1,0:T(8,128)(2,1)}) %all-gather.5.cloned.1.call-update) | async-done | bytes 8388624 | tf_op jit(solution)/shard_map/all_gather | solution.py:26
  197.8 0.0 copy-start
  197.8 10.5 %multiply_negate_fusion = (f32[1024,512]{1,0:T(8,128)}, bf16[1024,512]{1,0:T(8,128)(2,1)S(1)}) fusion(f32[]{:T(128)} %bitcast.41, f32[1024,512]{1,0:T(8,128)S(1)} %get-tuple-element.7, bf16[1,4096,512]{2,1,0:T(8,128)(2,1)} %all-gather.3.cloned.1.call-done, bf16[1,1024,4096]{2,1,0:T(8,128)(2,1)} %all-gather.5.cloned.1.call-done), kind=kOutput, calls=%fused_computation.5 | convolution fusion | flops 4297588736 | bytes 17825796 | tf_op jit(solution)/shard_map/pij,pjk->pik/dot_general | solution.py:27
  208.3 0.0 copy-done
  208.3 0.7 fusion.8
  209.0 0.1 copy.16
  209.2 0.0 copy-start.1
  209.2 1.0 copy-done.1
  210.2 0.0 reduce-scatter.8.cloned.1.call-update
  210.2 0.0 reduce-scatter.10.cloned.1.call-start
  210.2 24.9 %reduce-scatter.8.cloned.1.call-done = f32[128,512]{0,1:T(8,128)} async-done(((f32[512,512]{0,1:T(8,128)}), f32[128,512]{0,1:T(8,128)}) %reduce-scatter.8.cloned.1.call-update) | async-done | bytes 262160 | tf_op jit(solution)/shard_map/reduce_scatter | solution.py:52
  235.2 1.8 copy.14
  236.9 0.0 reduce-scatter.10.cloned.1.call-update
  237.0 0.0 reduce-scatter.6.cloned.1.call-start
  237.0 0.5 reduce-scatter.6.cloned.1.call-update
  237.6 20.3 %reduce-scatter.10.cloned.1.call-done = f32[32,512]{1,0:T(8,128)} async-done(((f32[128,512]{1,0:T(8,128)}), f32[32,512]{1,0:T(8,128)}) %reduce-scatter.10.cloned.1.call-update) | async-done | bytes 65552
  257.9 32.4 %reduce-scatter.6.cloned.1.call-done = f32[256,512]{1,0:T(8,128)} async-done(((f32[1024,512]{1,0:T(8,128)}), f32[256,512]{1,0:T(8,128)}) %reduce-scatter.6.cloned.1.call-update) | async-done | bytes 524304 | tf_op jit(solution)/shard_map/reduce_scatter | solution.py:51
  (3 shorter events, 0.1 us)
Async XLA Ops:
  7.2 86.6 %all-gather.3.cloned.1.call-start = ((), (), s32[]{:S(2)}) async-start(), calls=%async_computation.3 | async-start | bytes 5242880 | tf_op jit(solution)/shard_map/all_gather | solution.py:30
  10.2 1.5 copy-start.2
  10.2 187.7 %all-gather.5.cloned.1.call-start = ((), (), s32[]{:S(2)}) async-start(), calls=%async_computation.4 | async-start | bytes 12582912 | tf_op jit(solution)/shard_map/all_gather | solution.py:26
  10.9 224.2 %reduce-scatter.8.cloned.1.call-start = ((), (), s32[]{:S(2)}) async-start(), calls=%async_computation.6 | async-start | bytes 1310720 | tf_op jit(solution)/shard_map/reduce_scatter | solution.py:52
  197.8 10.5 %copy-start = (bf16[1,1024,512]{2,1,0:T(8,128)(2,1)S(1)}, bf16[1,1024,512]{2,1,0:T(8,128)(2,1)}, u32[]{:S(2)}) copy-start(bf16[1,1024,512]{2,1,0:T(8,128)(2,1)} %get-tuple-element.6) | copy-start | bytes 3145732
  209.2 1.0 copy-start.1
  210.2 47.7 %reduce-scatter.10.cloned.1.call-start = ((), (), s32[]{:S(2)}) async-start(), calls=%async_computation.7 | async-start | bytes 327680
  237.0 53.3 %reduce-scatter.6.cloned.1.call-start = ((), (), s32[]{:S(2)}) async-start(), calls=%async_computation.5 | async-start | bytes 2621440 | tf_op jit(solution)/shard_map/reduce_scatter | solution.py:51
Sparse Core Ops, SparseCore 0:
  10.3 83.4 all-gather.2
  95.3 102.4 all-gather.4
  210.3 24.8 reduce-scatter.7
  237.8 19.9 reduce-scatter.9
  260.8 29.4 reduce-scatter.5
where the time goes:
time: 297 us
  waiting for transfers between devices  265 us (89%)
  between operations  14.5 us (5%)
  matrix products  14.1 us (5%)
    all_gather x1, waiting for transfers between devices, body(): whole_rows = lax.all_gather(green, 'col', axis=2, tiled=True)  104 us
    all_gather x1, waiting for transfers between devices, body(): lax.all_gather(masked, 'row', axis=1, tiled=True)  82 us
    reduce_scatter x1, waiting for transfers between devices, body(): lax.psum_scatter(off_term, 'pole', scatter_dimension=0, tiled=True)  32.4 us
    reduce_scatter x1, waiting for transfers between devices, body(): lax.psum_scatter(diag_term, 'pole', scatter_dimension=0, tiled=True)  24.9 us
    unnamed x6, waiting for transfers between devices  21.6 us
    dot_general x1, matrix products, body(): jnp.einsum('pij,pjk->pik', whole_rows, lax.all_gather(masked, 'row', axis...  10.5 us
  transfers between devices with their start and end apart: 5, of which 5 were waited for; matrix products, arithmetic and copies ran while one was open for 0% of the time, Pallas kernels for 0%

commit v1 on v0

--- a/solution.py
+++ b/solution.py
@@ -5,6 +5,24 @@
 
 BLOCK = 512
 ANC = 8
+
+
+def gather_around(value, axis, dim):
+    ways, here, step = (lax.axis_size(axis), lax.axis_index(axis), value.shape[dim])
+    shape = [n * ways if d == dim else n for d, n in enumerate(value.shape)]
+    full = lax.dynamic_update_slice_in_dim(
+        jnp.zeros(shape, value.dtype), value, here * step, axis=dim
+    )
+    going_up = going_down = value
+    for far in range(1, ways // 2 + 1):
+        going_up = lax.ppermute(going_up, axis, [(d, (d + 1) % ways) for d in range(ways)])
+        full = lax.dynamic_update_slice_in_dim(full, going_up, (here - far) % ways * step, axis=dim)
+        if 2 * far < ways:
+            going_down = lax.ppermute(going_down, axis, [(d, (d - 1) % ways) for d in range(ways)])
+            full = lax.dynamic_update_slice_in_dim(
+                full, going_down, (here + far) % ways * step, axis=dim
+            )
+    return full
 
 
 def body(green, factor, diag_inverse, pole_weight, pattern):
@@ -27,7 +45,7 @@
     product = jnp.einsum(
         "pij,pjk->pik",
         whole_rows,
-        lax.all_gather(masked, "row", axis=1, tiled=True),
+        gather_around(masked, "row", 1),
         preferred_element_type=jnp.float32,
     )
     update = (product * keep_mask[None]).astype(jnp.bfloat16)

time: 297 us -> 216 us (0.73)
  waiting for transfers between devices: 265 us -> 171 us
  local copies, waits for them, and re-layouts: 2.95 us -> 10.8 us
  starting transfers between devices: 0.2 us -> 5.16 us
    all_gather x1 -> x0, waiting for transfers between devices: 82 us -> none  [body(): lax.all_gather(masked, 'row', axis=1, tiled=True)]
    all_gather x1, waiting for transfers between devices: 104 us -> 28.2 us  [body(): whole_rows = lax.all_gather(green, 'col', axis=2, tiled=True)]
    ppermute x0 -> x3, waiting for transfers between devices: none -> 64.3 us  [the longest x2 44.9 us: gather_around(): lax.ppermute(going_up, axis, [(d, (d + 1) % ways) for d in range(ways)])]
    dynamic_update_slice x0 -> x3, local copies, waits for them, and re-layouts: none -> 5.61 us  [the longest x2 3.36 us: gather_around(): lax.dynamic_update_slice_in_dim(full, going_up, (here - far) % ways * ste...]
    ppermute x0 -> x3, starting transfers between devices: none -> 5 us  [the longest x2 2.96 us: gather_around(): lax.ppermute(going_up, axis, [(d, (d + 1) % ways) for d in range(ways)])]
    unnamed x6 -> x5, waiting for transfers between devices: 21.6 us -> 21.7 us
  transfers between devices with their start and end apart: 5 -> 7, of which waited for: 5 -> 7; matrix products, arithmetic and copies ran while one was open for 0% -> 5% of each run, Pallas kernels for 0% -> 0%
where the time goes in v1:
time: 216 us; the launch traced here: 215 us
  waiting for transfers between devices  171 us (79%)
  between operations  14.5 us (7%)
  matrix products  13.3 us (6%)
  local copies, waits for them, and re-layouts  10.8 us (5%)
  starting transfers between devices  5.16 us (2%)
    ppermute x2, waiting for transfers between devices, gather_around(): lax.ppermute(going_up, axis, [(d, (d + 1) % ways) for d in range(ways)])  44.9 us
    reduce_scatter x1, waiting for transfers between devices, body(): lax.psum_scatter(off_term, 'pole', scatter_dimension=0, tiled=True)  32.4 us
    all_gather x1, waiting for transfers between devices, body(): whole_rows = lax.all_gather(green, 'col', axis=2, tiled=True)  28.2 us
    reduce_scatter x1, waiting for transfers between devices, body(): lax.psum_scatter(diag_term, 'pole', scatter_dimension=0, tiled=True)  24.9 us
    unnamed x5, waiting for transfers between devices  21.7 us
    ppermute x1, waiting for transfers between devices, gather_around(): lax.ppermute(going_down, axis, [(d, (d - 1) % ways) for d in range(ways)])  19.5 us
    dot_general x1, matrix products, body(): jnp.einsum('pij,pjk->pik', whole_rows, gather_around(masked, 'row', 1), p...  10.5 us
  transfers between devices with their start and end apart: 7, of which 7 were waited for; matrix products, arithmetic and copies ran while one was open for 5% of the time, Pallas kernels for 0%

profile of v1, /device:TPU:0, one launch (start us, length us, event | category | flops | bytes accessed | tf_op | source)
XLA Modules:
  0.0 215.4 jit_solution(11737593502819178949)
XLA Ops:
  7.2 0.0 copy-start.1
  7.2 0.0 copy-start.4
  7.2 0.0 all-gather.2.cloned.1.call-start
  7.2 0.7 all-gather.2.cloned.1.call-update
  7.9 0.0 reduce-scatter.8.cloned.1.call-start
  8.0 0.0 copy-start.3
  8.0 2.2 %broadcast.96 = bf16[4096,512]{1,0:T(8,128)(2,1)} broadcast(bf16[]{:T(256)} %constant.60.clone.1), dimensions={} | broadcast | bytes 4194306 | tf_op jit(solution)/shard_map/broadcast.33
  10.3 2.1 bitcast_dynamic-update-slice_fusion.3
  12.4 3.0 %collective-permute-start = (bf16[1,1024,512]{2,1,0:T(8,128)(2,1)}, bf16[1,1024,512]{2,1,0:T(8,128)(2,1)S(1)}, u32[]{:S(2)}, u32[]{:S(2)}) collective-permute-start(bf16[1,1024,512]{2,1,0:T(8,128)(2,1)} %get-tuple-element.7), channel_id=1, source_target_pairs={{0,2},{2,4},{4,6},{6,0},{1,3},{3,5},{5,7},{7,1},{8,10},{10,12},{12... | collective-permute-start | bytes 3145736 | tf_op jit(solution)/shard_map/ppermute | solution.py:18
  15.3 2.0 collective-permute-start.1
  17.4 24.3 %collective-permute-done = bf16[1,1024,512]{2,1,0:T(8,128)(2,1)S(1)} collective-permute-done((bf16[1,1024,512]{2,1,0:T(8,128)(2,1)}, bf16[1,1024,512]{2,1,0:T(8,128)(2,1)S(1)}, u32[]{:S(2)}, u32[]{:S(2)}) %collective-permute-start) | collective-permute-done | bytes 1048608 | tf_op jit(solution)/shard_map/ppermute | solution.py:18
  41.6 0.0 collective-permute-start.2
  42.3 0.1 copy.11
  42.4 1.1 bitcast_dynamic-update-slice_fusion.2
  43.5 19.5 %collective-permute-done.1 = bf16[1,1024,512]{2,1,0:T(8,128)(2,1)} collective-permute-done((bf16[1,1024,512]{2,1,0:T(8,128)(2,1)}, bf16[1,1024,512]{2,1,0:T(8,128)(2,1)}, u32[]{:S(2)}, u32[]{:S(2)}) %collective-permute-start.1) | collective-permute-done | bytes 1048608 | tf_op jit(solution)/shard_map/ppermute | solution.py:21
  63.0 2.3 %bitcast_dynamic-update-slice_fusion.1 = bf16[4096,512]{1,0:T(8,128)(2,1)} fusion(bf16[4096,512]{1,0:T(8,128)(2,1)} %bitcast_dynamic-update-slice_fusion.2, s32[]{:T(128)S(6)} %select_n.55, bf16[1,1024,512]{2,1,0:T(8,128)(2,1)} %collective-permute-done.1), kind=kLoop, calls=%fused_computation.10 | loop fusion | bytes 2097156 | tf_op jit(solution)/shard_map/dynamic_update_slice | solution.py:22
  65.2 20.6 %collective-permute-done.2 = bf16[1,1024,512]{2,1,0:T(8,128)(2,1)} collective-permute-done((bf16[1,1024,512]{2,1,0:T(8,128)(2,1)S(1)}, bf16[1,1024,512]{2,1,0:T(8,128)(2,1)}, u32[]{:S(2)}, u32[]{:S(2)}) %collective-permute-start.2) | collective-permute-done | bytes 1048608 | tf_op jit(solution)/shard_map/ppermute | solution.py:18
  85.8 2.3 %bitcast_dynamic-update-slice_fusion = bf16[4096,512]{1,0:T(8,128)(2,1)} fusion(bf16[4096,512]{1,0:T(8,128)(2,1)} %bitcast_dynamic-update-slice_fusion.1, s32[]{:T(128)S(6)} %select_n.57, bf16[1,1024,512]{2,1,0:T(8,128)(2,1)} %collective-permute-done.2), kind=kLoop, calls=%fused_computation.9 | loop fusion | bytes 2097156 | tf_op jit(solution)/shard_map/dynamic_update_slice | solution.py:19
  88.1 28.2 %all-gather.2.cloned.1.call-done = bf16[1,1024,4096]{2,1,0:T(8,128)(2,1)} async-done(((bf16[1,1024,2048]{2,1,0:T(8,128)(2,1)}), bf16[1,1024,4096]{2,1,0:T(8,128)(2,1)}) %all-gather.2.cloned.1.call-update) | async-done | bytes 8388624 | tf_op jit(solution)/shard_map/all_gather | solution.py:44
  116.3 10.5 %multiply_negate_fusion = (f32[1024,512]{1,0:T(8,128)}, bf16[1024,512]{1,0:T(8,128)(2,1)S(1)}) fusion(f32[]{:T(128)} %bitcast.43, f32[1024,512]{1,0:T(8,128)S(1)} %get-tuple-element.8, bf16[4096,512]{1,0:T(8,128)(2,1)} %bitcast_dynamic-update-slice_fusion, bf16[1,1024,4096]{2,1,0:T(8,128)(2,1)} %all-gather.2.cloned.1.call-done), kind=kOutput, calls=%fused_computation.4 | convolution fusion | flops 4297588736 | bytes 17825796 | tf_op jit(solution)/shard_map/pij,pjk->pik/dot_general | solution.py:45
  126.8 0.7 fusion.5
  127.5 0.1 copy.20
  127.7 1.0 copy-done
  128.6 0.0 reduce-scatter.8.cloned.1.call-update
  128.6 0.0 reduce-scatter.10.cloned.1.call-start
  128.7 24.9 %reduce-scatter.8.cloned.1.call-done = f32[128,512]{0,1:T(8,128)} async-done(((f32[512,512]{0,1:T(8,128)}), f32[128,512]{0,1:T(8,128)}) %reduce-scatter.8.cloned.1.call-update) | async-done | bytes 262160 | tf_op jit(solution)/shard_map/reduce_scatter | solution.py:70
  153.6 1.8 copy.14
  155.4 0.0 reduce-scatter.10.cloned.1.call-update
  155.4 0.0 reduce-scatter.6.cloned.1.call-start
  155.4 0.5 reduce-scatter.6.cloned.1.call-update
  156.0 20.5 %reduce-scatter.10.cloned.1.call-done = f32[32,512]{1,0:T(8,128)} async-done(((f32[128,512]{1,0:T(8,128)}), f32[32,512]{1,0:T(8,128)}) %reduce-scatter.10.cloned.1.call-update) | async-done | bytes 65552
  176.4 32.4 %reduce-scatter.6.cloned.1.call-done = f32[256,512]{1,0:T(8,128)} async-done(((f32[1024,512]{1,0:T(8,128)}), f32[256,512]{1,0:T(8,128)}) %reduce-scatter.6.cloned.1.call-update) | async-done | bytes 524304 | tf_op jit(solution)/shard_map/reduce_scatter | solution.py:69
  (9 shorter events, 0.1 us)
Async XLA Ops:
  7.2 3.1 %copy-start.1 = (bf16[1,1024,512]{2,1,0:T(8,128)(2,1)S(1)}, bf16[1,1024,512]{2,1,0:T(8,128)(2,1)}, u32[]{:S(2)}) copy-start(bf16[1,1024,512]{2,1,0:T(8,128)(2,1)} %param.6) | copy-start | bytes 3145732
  7.2 3.1 %copy-start.4 = (s32[8,2]{0,1:T(2,128)S(1)}, s32[8,2]{0,1:T(2,128)}, u32[]{:S(2)}) copy-start(s32[8,2]{0,1:T(2,128)} %param.9) | copy-start | bytes 196
  7.2 109.1 %all-gather.2.cloned.1.call-start = ((), (), s32[]{:S(2)}) async-start(), calls=%async_computation.3 | async-start | bytes 12582912 | tf_op jit(solution)/shard_map/all_gather | solution.py:44
  7.9 145.7 %reduce-scatter.8.cloned.1.call-start = ((), (), s32[]{:S(2)}) async-start(), calls=%async_computation.5 | async-start | bytes 1310720 | tf_op jit(solution)/shard_map/reduce_scatter | solution.py:70
  8.0 34.3 %copy-start.3 = (bf16[1,128,512]{2,1,0:T(8,128)(2,1)S(1)}, bf16[1,128,512]{2,1,0:T(8,128)(2,1)}, u32[]{:S(2)}) copy-start(bf16[1,128,512]{2,1,0:T(8,128)(2,1)} %param.7) | copy-start | bytes 393220
  12.4 29.3 %collective-permute-start = (bf16[1,1024,512]{2,1,0:T(8,128)(2,1)}, bf16[1,1024,512]{2,1,0:T(8,128)(2,1)S(1)}, u32[]{:S(2)}, u32[]{:S(2)}) collective-permute-start(bf16[1,1024,512]{2,1,0:T(8,128)(2,1)} %get-tuple-element.7), channel_id=1, source_target_pairs={{0,2},{2,4},{4,6},{6,0},{1,3},{3,5},{5,7},{7,1},{8,10},{10,12},{12... | collective-permute-start | bytes 3145736 | tf_op jit(solution)/shard_map/ppermute | solution.py:18
  15.3 47.6 %collective-permute-start.1 = (bf16[1,1024,512]{2,1,0:T(8,128)(2,1)}, bf16[1,1024,512]{2,1,0:T(8,128)(2,1)}, u32[]{:S(2)}, u32[]{:S(2)}) collective-permute-start(bf16[1,1024,512]{2,1,0:T(8,128)(2,1)} %get-tuple-element.7), channel_id=1, source_target_pairs={{0,6},{2,0},{4,2},{6,4},{1,7},{3,1},{5,3},{7,5},{8,14},{10,8},{12,... | collective-permute-start | bytes 3145736 | tf_op jit(solution)/shard_map/ppermute | solution.py:21
  41.6 44.2 %collective-permute-start.2 = (bf16[1,1024,512]{2,1,0:T(8,128)(2,1)S(1)}, bf16[1,1024,512]{2,1,0:T(8,128)(2,1)}, u32[]{:S(2)}, u32[]{:S(2)}) collective-permute-start(bf16[1,1024,512]{2,1,0:T(8,128)(2,1)S(1)} %collective-permute-done), channel_id=1, source_target_pairs={{0,2},{2,4},{4,6},{6,0},{1,3},{3,5},{5,7},{7,1},{8,10},{10,12},{12... | collective-permute-start | bytes 3145736 | tf_op jit(solution)/shard_map/ppermute | solution.py:18
  116.3 10.5 %copy-start.2 = (bf16[1,1024,512]{2,1,0:T(8,128)(2,1)S(1)}, bf16[1,1024,512]{2,1,0:T(8,128)(2,1)}, u32[]{:S(2)}) copy-start(bf16[1,1024,512]{2,1,0:T(8,128)(2,1)} %get-tuple-element.7) | copy-start | bytes 3145732
  127.7 1.0 copy-start
  128.6 47.8 %reduce-scatter.10.cloned.1.call-start = ((), (), s32[]{:S(2)}) async-start(), calls=%async_computation.6 | async-start | bytes 327680
  155.4 53.4 %reduce-scatter.6.cloned.1.call-start = ((), (), s32[]{:S(2)}) async-start(), calls=%async_computation.4 | async-start | bytes 2621440 | tf_op jit(solution)/shard_map/reduce_scatter | solution.py:69
Sparse Core Ops, SparseCore 0:
  9.5 106.6 all-gather.1
  128.8 24.7 reduce-scatter.7
  156.4 19.9 reduce-scatter.9
  179.4 29.3 reduce-scatter.5
